TPU v7x, 32 devices: a whole 2x2x4 slice. The times are simulated.
32 devices in a mesh: dp: 4 (over y, x), proto: 4 (over z), pair: 2 (over core).
Axes of the slice: x: 2, y: 2, z: 4, core: 2. Of those that a mesh axis runs over, the one named last changes fastest.
Arguments:
- student_patches: bfloat16 [2, 4096, 256], P('pair', 'dp'), may hold values from -2 to 2
- teacher_patches: bfloat16 [2, 4096, 256], P('pair', 'dp'), may hold values from -8 to 8
- student_proto: bfloat16 [65536, 256], P('proto'), may hold values from -4 to 4
- teacher_proto: bfloat16 [65536, 256], P('proto'), may hold values from -4 to 4
- masked_rows: int32 [2, 1024], P('pair', 'dp'), may hold values from 0 to 1023, as said below
Outputs:
- student_grad: float32 [2, 1024, 256], P('pair', 'dp')
Inputs may be any that keep to these rules, and one draw needn't show every extreme that they name: `masked_rows`: entries of one device's block name distinct patch rows of that device's 4 images (image g owns rows g * 256 to (g + 1) * 256 - 1); every image has between 16 and 112 masked patches.
All inputs are finite; a program needn't handle non-finite values.
Results may differ from a plain program's by a relative error of at most 0.00075.
The roundings to bfloat16 on the way count: a program that leaves them out, or rounds other values in their place, can miss the bound.
Values sent between devices are 32-bit elements; how exact they have to be, the bound alone decides.
No kernel may reach another device: no remote copies, remote signals or barrier semaphores. Data moves between devices by JAX's collectives and lax.ppermute only.
A program may use at most 128 MiB of HBM per device.

v0:
```python
import jax
import jax.numpy as jnp
from jax import lax
from jax.sharding import PartitionSpec as P

PATCHES = 256
ITERS = 2
teacher_temp = 0.07
student_temp = 0.1
epsilon = 1e-06


def inverse_norms(matrix):
    return lax.rsqrt(jnp.sum(jnp.square(matrix.astype(jnp.float32)), axis=-1) + epsilon)


def scores_of(features, protos):
    return lax.dot_general(
        features, protos, (((1,), (1,)), ((), ())), preferred_element_type=jnp.float32
    )


def on_device(student_patches, teacher_patches, student_proto, teacher_proto, masked_rows):
    slot_rows = masked_rows[0]
    count_slots = slot_rows.shape[0]
    images = student_patches.shape[1] // PATCHES
    image_of = slot_rows // PATCHES
    member = (image_of[:, None] == jnp.arange(images, dtype=jnp.int32)[None, :]).astype(jnp.float32)
    per_image = jnp.sum(member, axis=0)
    slot_count = jnp.sum(member * per_image[None, :], axis=1)
    weights = count_slots / images / slot_count
    student_rows = jnp.take(student_patches[0], slot_rows, axis=0)
    teacher_rows = jnp.take(teacher_patches[0], slot_rows, axis=0)
    teacher_scale = inverse_norms(teacher_proto)
    student_scale = inverse_norms(student_proto)
    teacher_inv = inverse_norms(teacher_rows)
    teacher_exp = jnp.exp(
        scores_of(teacher_rows, teacher_proto)
        * teacher_inv[:, None]
        * teacher_scale[None, :]
        / teacher_temp
    )
    row_factor = jnp.ones((count_slots,), jnp.float32)
    column_factor = jnp.ones((teacher_proto.shape[0],), jnp.float32)
    for sweep in range(ITERS):
        column_part = jnp.dot(row_factor, teacher_exp, precision=lax.Precision.HIGHEST)
        column_factor = 1.0 / lax.psum(column_part, ("dp", "pair"))
        row_part = jnp.dot(teacher_exp, column_factor, precision=lax.Precision.HIGHEST)
        row_factor = 1.0 / lax.psum(row_part, "proto")
    targets = (teacher_exp * row_factor[:, None] * (column_factor * student_scale)[None, :]).astype(
        jnp.bfloat16
    )
    student_inv = inverse_norms(student_rows)
    student_exp = jnp.exp(
        scores_of(student_rows, student_proto)
        * student_inv[:, None]
        * student_scale[None, :]
        / student_temp
    )
    partition_part = jnp.sum(student_exp, axis=1)
    partition = lax.psum(partition_part, "proto")
    pushed_w = (student_exp * student_scale[None, :]).astype(jnp.bfloat16)
    pushed = jnp.dot(pushed_w, student_proto, preferred_element_type=jnp.float32)
    pulled = jnp.dot(targets, student_proto, preferred_element_type=jnp.float32)
    pushed, pulled = lax.psum((pushed, pulled), "proto")
    inner_grad = (pushed / partition[:, None] - pulled) / student_temp
    rows_float = student_rows.astype(jnp.float32)
    row_dot = jnp.sum(rows_float * inner_grad, axis=1)
    cube = student_inv * student_inv * student_inv
    result_grad = weights[:, None] * (
        student_inv[:, None] * inner_grad - rows_float * (cube * row_dot)[:, None]
    )
    return result_grad[None]


def solution(mesh):
    placed = (
        P("pair", "dp", None),
        P("pair", "dp", None),
        P("proto", None),
        P("proto", None),
        P("pair", "dp"),
    )
    return jax.shard_map(
        on_device, mesh=mesh, in_specs=placed, out_specs=P("pair", "dp", None), check_vma=False
    )
```

profile of v0, /device:TPU:0, one launch (start us, length us, event | category | flops | bytes accessed | tf_op | source)
XLA Modules:
  0.0 296.8 jit_solution(648709590151249231)
XLA Ops:
  6.5 0.0 all-reduce.6.cloned.1.call-start
  6.5 0.7 compare_and_fusion
  7.3 0.7 and_select_fusion
  8.0 5.2 %multiply_reduce_fusion = f32[16384]{0:T(1024)S(1)} fusion(bf16[16384,256]{1,0:T(8,128)(2,1)} %param.10), kind=kLoop, calls=%fused_computation.11 | loop fusion | flops 12566528 | bytes 8454144 | tf_op jit(solution)/shard_map/reduce_sum | solution.py:14
  13.2 1.2 gather_fusion
  14.4 2.1 gather_fusion.1
  16.5 0.2 fusion.11
  16.7 12.4 %fusion.2 = f32[256,16384]{1,0:T(8,128)} fusion(bf16[16384,256]{1,0:T(8,128)(2,1)} %param.10, f32[16384]{0:T(1024)S(1)} %add_rsqrt_fusion, f32[256]{0:T(256)S(1)} %add_rsqrt_fusion.2, bf16[256,256]{1,0:T(8,128)(2,1)S(1)} %gather_fusion.1, pred[256]{0:T(512)(128)(4,1)S(1)} %compare_and_fusion), kind=kOutput, calls=%fused_computation.5 | convolution fusion | flops 2160132096 | bytes 25363712 | tf_op jit(solution)/shard_map/dot_general | solution.py:18
  29.1 12.1 %fusion.17 = f32[1,16384]{1,0:T(1,128)} fusion(f32[256,16384]{1,0:T(8,128)} %fusion.2), kind=kOutput, calls=%fused_computation.49 | convolution fusion | flops 50331648 | bytes 16842752 | tf_op jit(solution)/shard_map/dot_general | solution.py:46
  41.1 0.0 all-reduce.6.cloned.1.call-update
  41.2 0.2 all-reduce.8.cloned.1.call-start
  41.4 5.2 %multiply_reduce_fusion.1 = f32[16384]{0:T(1024)S(1)} fusion(bf16[16384,256]{1,0:T(8,128)(2,1)} %param.9), kind=kLoop, calls=%fused_computation.13 | loop fusion | flops 12566528 | bytes 8454144 | tf_op jit(solution)/shard_map/reduce_sum | solution.py:14
  46.6 50.6 %all-reduce.6.cloned.1.call-done = f32[16384]{0:T(1024)} async-done(((f32[16384]{0:T(1024)}), f32[16384]{0:T(1024)}) %all-reduce.6.cloned.1.call-update) | async-done | bytes 65552 | tf_op jit(solution)/shard_map/psum | solution.py:47
  97.2 0.9 broadcast_divide_fusion.1
  98.1 16.1 %fusion.23 = f32[1,256]{1,0:T(1,128)S(1)} fusion(f32[256,16384]{1,0:T(8,128)} %fusion.2, f32[16384,1]{0,1:T(1,128)S(1)} %bitcast.28), kind=kOutput, calls=%fused_computation.59 | convolution fusion | flops 50331648 | bytes 16843776 | tf_op jit(solution)/shard_map/dot_general | solution.py:48
  114.1 11.7 %psum.52 = f32[256]{0:T(256)S(1)} all-reduce(f32[256]{0:T(256)S(1)} %bitcast.30), channel_id=1, replica_groups=mesh['dp'=4,'proto'=4,'pair'=2] {'proto'}, use_global_device_ids=true, to_apply=%region_10.12 | all-reduce | flops 256 | bytes 2048 | tf_op jit(solution)/shard_map/psum | solution.py:49
  125.8 12.1 %fusion.24 = f32[1,16384]{1,0:T(1,128)} fusion(f32[256,1]{0,1:T(1,128)S(1)} %bitcast.31, f32[256,16384]{1,0:T(8,128)} %fusion.2), kind=kOutput, calls=%fused_computation.60 | convolution fusion | flops 50331648 | bytes 16843776 | tf_op jit(solution)/shard_map/dot_general | solution.py:46
  137.9 0.0 all-reduce.8.cloned.1.call-update
  137.9 0.3 all-reduce.10.cloned.1.call-start
  138.2 49.7 %all-reduce.8.cloned.1.call-done = f32[16384]{0:T(1024)} async-done(((f32[16384]{0:T(1024)}), f32[16384]{0:T(1024)}) %all-reduce.8.cloned.1.call-update) | async-done | bytes 65552 | tf_op jit(solution)/shard_map/psum | solution.py:47
  187.9 0.9 add_rsqrt_fusion.1
  188.8 16.1 %fusion.25 = f32[1,256]{1,0:T(1,128)S(1)} fusion(f32[256,16384]{1,0:T(8,128)} %fusion.2, f32[16384,1]{0,1:T(1,128)S(1)} %bitcast.25), kind=kOutput, calls=%fused_computation.61 | convolution fusion | flops 50331648 | bytes 16843776 | tf_op jit(solution)/shard_map/dot_general | solution.py:48
  204.8 12.6 %fusion.22 = (f32[256]{0:T(256)S(1)}, f32[256,16384]{1,0:T(8,128)}) fusion(f32[16384]{0:T(1024)S(1)} %get-tuple-element.12, f32[256]{0:T(256)S(1)} %add_rsqrt_fusion.3, bf16[16384,256]{1,0:T(8,128)(2,1)} %param.9, bf16[256,256]{1,0:T(8,128)(2,1)S(1)} %gather_fusion, pred[256]{0:T(512)(128)(4,1)S(1)} %compare_and_fusion), kind=kOutput, calls=%fused_computation.58 | convolution fusion | flops 2164326144 | bytes 25364736 | tf_op jit(solution)/shard_map/dot_general | solution.py:18
  217.5 11.7 %all-reduce = (f32[256]{0:T(256)S(1)}, f32[256]{0:T(256)S(1)}) all-reduce(f32[256]{0:T(256)S(1)} %bitcast.29, f32[256]{0:T(256)S(1)} %get-tuple-element.19), channel_id=1, replica_groups=mesh['dp'=4,'proto'=4,'pair'=2] {'proto'}, use_global_device_ids=true, to_apply=%region_12.14 | all-reduce | flops 512 | bytes 4096 | tf_op jit(solution)/shard_map/psum | solution.py:49
  229.1 11.2 %fusion.6 = f32[256,256]{1,0:T(8,128)} fusion(bf16[16384,256]{1,0:T(8,128)(2,1)} %param.9, f32[256,16384]{1,0:T(8,128)} %get-tuple-element.20, f32[16384]{0:T(1024)S(1)} %get-tuple-element.12), kind=kOutput, calls=%fused_computation.14 | convolution fusion | flops 2155872256 | bytes 25493504 | tf_op jit(solution)/shard_map/dot_general | solution.py:63
  240.3 11.2 %fusion.7 = f32[256,256]{1,0:T(8,128)} fusion(bf16[16384,256]{1,0:T(8,128)(2,1)} %param.9, f32[256,16384]{1,0:T(8,128)} %fusion.2, f32[16384]{0:T(1024)S(1)} %get-tuple-element.13, f32[256]{0:T(256)S(1)} %broadcast_divide_fusion.3), kind=kOutput, calls=%fused_computation.15 | convolution fusion | flops 2160066560 | bytes 25494528 | tf_op jit(solution)/shard_map/dot_general | solution.py:64
  251.6 0.0 all-reduce.10.cloned.1.call-update
  251.6 0.1 convert_reduce_fusion
  251.7 0.1 select_reduce_fusion
  251.8 35.3 %all-reduce.10.cloned.1.call-done = (f32[256,256]{1,0:T(8,128)}, f32[256,256]{1,0:T(8,128)}) async-done(((f32[256,256]{1,0:T(8,128)}, f32[256,256]{1,0:T(8,128)}), (f32[256,256]{1,0:T(8,128)}, f32[256,256]{1,0:T(8,128)})) %all-reduce.10.cloned.1.call-update) | async-done | bytes 524304 | tf_op jit(solution)/shard_map/psum | solution.py:65
  287.1 1.2 fusion.12
  288.3 2.0 fusion.15
  (10 shorter events, 0.1 us)
Async XLA Ops:
  6.5 6.7 %copy-start = (bf16[1,1024,256]{2,1,0:T(8,128)(2,1)S(1)}, bf16[1,1024,256]{2,1,0:T(8,128)(2,1)}, u32[]{:S(2)}) copy-start(bf16[1,1024,256]{2,1,0:T(8,128)(2,1)} %param.7) | copy-start | bytes 1572868
  6.5 90.7 %all-reduce.6.cloned.1.call-start = ((), (), s32[]{:S(2)}) async-start(), calls=%async_computation | async-start | bytes 131072 | tf_op jit(solution)/shard_map/psum | solution.py:47
  41.2 146.7 %all-reduce.8.cloned.1.call-start = ((), (), s32[]{:S(2)}) async-start(), calls=%async_computation.1 | async-start | bytes 131072 | tf_op jit(solution)/shard_map/psum | solution.py:47
  137.9 149.2 %all-reduce.10.cloned.1.call-start = ((), (), s32[]{:S(2)}) async-start(), calls=%async_computation.2 | async-start | bytes 1048576 | tf_op jit(solution)/shard_map/psum | solution.py:65
Sparse Core Ops, SparseCore 0:
  41.3 55.8 all-reduce.5
  138.0 49.8 all-reduce.7
  251.7 35.3 all-reduce.9
where the time goes:
time: 297 us
  waiting for transfers between devices  136 us (46%)
  matrix products  104 us (35%)
  blocking collectives  23.3 us (8%)
  other arithmetic  17.3 us (6%)
  between operations  13.2 us (4%)
  local copies, waits for them, and re-layouts  3.23 us (1%)
    psum x2, waiting for transfers between devices, on_device(): column_factor = 1.0 / lax.psum(column_part, ('dp', 'pair'))  100 us
    psum x1, waiting for transfers between devices, on_device(): pushed, pulled = lax.psum((pushed, pulled), 'proto')  35.3 us
    dot_general x2, matrix products, on_device(): jnp.dot(teacher_exp, column_factor, precision=lax.Precision.HIGHEST)  32.1 us
    dot_general x2, matrix products, scores_of(): lax.dot_general(features, protos, (((1,), (1,)), ((), ())), preferred_ele...  25 us
    dot_general x2, matrix products, on_device(): jnp.dot(row_factor, teacher_exp, precision=lax.Precision.HIGHEST)  24.1 us
    psum x2, blocking collectives, on_device(): row_factor = 1.0 / lax.psum(row_part, 'proto')  23.3 us
    dot_general x1, matrix products, on_device(): pulled = jnp.dot(targets, student_proto, preferred_element_type=jnp.float32)  11.2 us
    dot_general x1, matrix products, on_device(): jnp.dot(pushed_w, student_proto, preferred_element_type=jnp.float32)  11.2 us
  transfers between devices with their start and end apart: 3, of which 3 were waited for; matrix products, arithmetic and copies ran while one was open for 2% of the time, Pallas kernels for 0%

commit v1 on v0

--- a/solution.py
+++ b/solution.py
@@ -8,6 +8,11 @@
 teacher_temp = 0.07
 student_temp = 0.1
 epsilon = 1e-06
+
+
+def touch_series_all(frame, bus_axis):
+    long_array = lax.all_gather(frame, bus_axis).sum(axis=0)
+    return long_array
 
 
 def inverse_norms(matrix):
@@ -44,7 +49,7 @@
     column_factor = jnp.ones((teacher_proto.shape[0],), jnp.float32)
     for sweep in range(ITERS):
         column_part = jnp.dot(row_factor, teacher_exp, precision=lax.Precision.HIGHEST)
-        column_factor = 1.0 / lax.psum(column_part, ("dp", "pair"))
+        column_factor = 1.0 / touch_series_all(column_part, ("dp", "pair"))
         row_part = jnp.dot(teacher_exp, column_factor, precision=lax.Precision.HIGHEST)
         row_factor = 1.0 / lax.psum(row_part, "proto")
     targets = (teacher_exp * row_factor[:, None] * (column_factor * student_scale)[None, :]).astype(

time: 297 us -> 214 us (0.72)
  waiting for transfers between devices: 136 us -> 37.3 us
  blocking collectives: 23.3 us -> 41.8 us
    psum x2 -> x0, waiting for transfers between devices: 100 us -> none  [on_device(): column_factor = 1.0 / lax.psum(column_part, ('dp', 'pair'))]
    all_gather x0 -> x2, blocking collectives: none -> 21.5 us  [touch_series_all(): long_array = lax.all_gather(frame, bus_axis).sum(axis=0)]
    psum x2, blocking collectives: 23.3 us -> 20.3 us  [on_device(): row_factor = 1.0 / lax.psum(row_part, 'proto')]
  transfers between devices with their start and end apart: 3 -> 1, of which waited for: 3 -> 1; matrix products, arithmetic and copies ran while one was open for 2% -> 0% of each run, Pallas kernels for 0% -> 0%
where the time goes in v1:
time: 214 us; the launch traced here: 213 us
  matrix products  102 us (48%)
  blocking collectives  41.8 us (20%)
  waiting for transfers between devices  37.3 us (17%)
  other arithmetic  15.9 us (7%)
  between operations  13.5 us (6%)
  local copies, waits for them, and re-layouts  2.51 us (1%)
    psum x1, waiting for transfers between devices, on_device(): pushed, pulled = lax.psum((pushed, pulled), 'proto')  37.3 us
    dot_general x2, matrix products, on_device(): jnp.dot(teacher_exp, column_factor, precision=lax.Precision.HIGHEST)  32.1 us
    dot_general x2, matrix products, scores_of(): lax.dot_general(features, protos, (((1,), (1,)), ((), ())), preferred_ele...  25 us
    dot_general x2, matrix products, on_device(): jnp.dot(row_factor, teacher_exp, precision=lax.Precision.HIGHEST)  22.9 us
    all_gather x2, blocking collectives, touch_series_all(): long_array = lax.all_gather(frame, bus_axis).sum(axis=0)  21.5 us
    psum x2, blocking collectives, on_device(): row_factor = 1.0 / lax.psum(row_part, 'proto')  20.3 us
    dot_general x1, matrix products, on_device(): pulled = jnp.dot(targets, student_proto, preferred_element_type=jnp.float32)  11.2 us
    dot_general x1, matrix products, on_device(): jnp.dot(pushed_w, student_proto, preferred_element_type=jnp.float32)  11.2 us
  transfers between devices with their start and end apart: 1, of which 1 were waited for; matrix products, arithmetic and copies ran while one was open for 0% of the time, Pallas kernels for 0%

profile of v1, /device:TPU:0, one launch (start us, length us, event | category | flops | bytes accessed | tf_op | source)
XLA Modules:
  0.0 213.5 jit_solution(17437117129867329421)
XLA Ops:
  6.5 0.0 copy-start
  6.5 0.0 all-reduce.4.cloned.1.call-start
  6.5 0.8 compare_and_fusion
  7.3 0.7 and_select_fusion
  8.0 5.2 %multiply_reduce_fusion = f32[16384]{0:T(1024)S(1)} fusion(bf16[16384,256]{1,0:T(8,128)(2,1)} %param.10), kind=kLoop, calls=%fused_computation.11 | loop fusion | flops 12566528 | bytes 8454144 | tf_op jit(solution)/shard_map/reduce_sum | solution.py:19
  13.3 5.2 %multiply_reduce_fusion.1 = f32[16384]{0:T(1024)S(1)} fusion(bf16[16384,256]{1,0:T(8,128)(2,1)} %param.9), kind=kLoop, calls=%fused_computation.13 | loop fusion | flops 12566528 | bytes 8454144 | tf_op jit(solution)/shard_map/reduce_sum | solution.py:19
  18.5 0.0 copy-done
  18.5 1.2 gather_fusion
  19.7 1.2 gather_fusion.1
  20.8 0.2 fusion.11
  21.1 12.4 %fusion.2 = f32[256,16384]{1,0:T(8,128)} fusion(bf16[16384,256]{1,0:T(8,128)(2,1)} %param.10, f32[16384]{0:T(1024)S(1)} %add_rsqrt_fusion, f32[256]{0:T(256)S(1)} %get-tuple-element.21, bf16[256,256]{1,0:T(8,128)(2,1)S(1)} %gather_fusion.1, pred[256]{0:T(512)(128)(4,1)S(1)} %compare_and_fusion), kind=kOutput, calls=%fused_computation.5 | convolution fusion | flops 2160132096 | bytes 25363712 | tf_op jit(solution)/shard_map/dot_general | solution.py:23
  33.4 11.4 %fusion.17 = f32[1,16384]{1,0:T(1,128)S(1)} fusion(f32[256,16384]{1,0:T(8,128)} %fusion.2), kind=kOutput, calls=%fused_computation.49 | convolution fusion | flops 50331648 | bytes 16842752 | tf_op jit(solution)/shard_map/dot_general | solution.py:51
  44.9 11.5 %all-gather = f32[131072]{0:T(1024)S(1)} all-gather(f32[16384]{0:T(1024)S(1)} %bitcast.27), channel_id=2, replica_groups=mesh['dp'=4,'proto'=4,'pair'=2] {'dp','pair'}, dimensions={0}, use_global_device_ids=true | all-gather | bytes 589824 | tf_op jit(solution)/shard_map/all_gather | solution.py:14
  56.4 0.1 reshape.84
  56.5 0.1 reduce_sum.97
  56.6 16.1 %fusion.23 = f32[1,256]{1,0:T(1,128)S(1)} fusion(f32[256,16384]{1,0:T(8,128)} %fusion.2, f32[16384,1]{0,1:T(1,128)S(1)} %bitcast.28), kind=kOutput, calls=%fused_computation.59 | convolution fusion | flops 50331648 | bytes 16843776 | tf_op jit(solution)/shard_map/dot_general | solution.py:53
  72.7 12.0 %psum.37 = f32[256]{0:T(256)S(1)} all-reduce(f32[256]{0:T(256)S(1)} %bitcast.30), channel_id=1, replica_groups=mesh['dp'=4,'proto'=4,'pair'=2] {'proto'}, use_global_device_ids=true, to_apply=%region_10.12 | all-reduce | flops 256 | bytes 2048 | tf_op jit(solution)/shard_map/psum | solution.py:54
  84.7 11.4 %fusion.24 = f32[1,16384]{1,0:T(1,128)S(1)} fusion(f32[256,1]{0,1:T(1,128)S(1)} %bitcast.31, f32[256,16384]{1,0:T(8,128)} %fusion.2), kind=kOutput, calls=%fused_computation.60 | convolution fusion | flops 50331648 | bytes 16843776 | tf_op jit(solution)/shard_map/dot_general | solution.py:51
  96.1 10.0 %all-gather.1 = f32[131072]{0:T(1024)S(1)} all-gather(f32[16384]{0:T(1024)S(1)} %bitcast.26), channel_id=3, replica_groups=mesh['dp'=4,'proto'=4,'pair'=2] {'dp','pair'}, dimensions={0}, use_global_device_ids=true | all-gather | bytes 589824 | tf_op jit(solution)/shard_map/all_gather | solution.py:14
  106.1 0.1 reshape.85
  106.2 0.1 reduce_sum.98
  106.4 16.1 %fusion.25 = f32[1,256]{1,0:T(1,128)S(1)} fusion(f32[256,16384]{1,0:T(8,128)} %fusion.2, f32[16384,1]{0,1:T(1,128)S(1)} %bitcast.25), kind=kOutput, calls=%fused_computation.61 | convolution fusion | flops 50331648 | bytes 16843776 | tf_op jit(solution)/shard_map/dot_general | solution.py:53
  122.5 12.6 %fusion.22 = (f32[256]{0:T(256)S(1)}, f32[256,16384]{1,0:T(8,128)}) fusion(f32[16384]{0:T(1024)S(1)} %get-tuple-element.12, f32[256]{0:T(256)S(1)} %get-tuple-element.22, bf16[16384,256]{1,0:T(8,128)(2,1)} %param.9, bf16[256,256]{1,0:T(8,128)(2,1)S(1)} %gather_fusion, pred[256]{0:T(512)(128)(4,1)S(1)} %compare_and_fusion), kind=kOutput, calls=%fused_computation.58 | convolution fusion | flops 2164326144 | bytes 25364736 | tf_op jit(solution)/shard_map/dot_general | solution.py:23
  135.1 8.3 %all-reduce = (f32[256]{0:T(256)S(1)}, f32[256]{0:T(256)S(1)}) all-reduce(f32[256]{0:T(256)S(1)} %bitcast.29, f32[256]{0:T(256)S(1)} %get-tuple-element.19), channel_id=1, replica_groups=mesh['dp'=4,'proto'=4,'pair'=2] {'proto'}, use_global_device_ids=true, to_apply=%region_12.14 | all-reduce | flops 512 | bytes 4096 | tf_op jit(solution)/shard_map/psum | solution.py:54
  143.5 11.2 %fusion.6 = f32[256,256]{1,0:T(8,128)} fusion(bf16[16384,256]{1,0:T(8,128)(2,1)} %param.9, f32[256,16384]{1,0:T(8,128)} %get-tuple-element.20, f32[16384]{0:T(1024)S(1)} %get-tuple-element.12), kind=kOutput, calls=%fused_computation.14 | convolution fusion | flops 2155872256 | bytes 25493504 | tf_op jit(solution)/shard_map/dot_general | solution.py:68
  154.7 11.2 %fusion.7 = f32[256,256]{1,0:T(8,128)} fusion(bf16[16384,256]{1,0:T(8,128)(2,1)} %param.9, f32[256,16384]{1,0:T(8,128)} %fusion.2, f32[16384]{0:T(1024)S(1)} %get-tuple-element.13, f32[256]{0:T(256)S(1)} %broadcast_divide_fusion.3), kind=kOutput, calls=%fused_computation.15 | convolution fusion | flops 2160066560 | bytes 25494528 | tf_op jit(solution)/shard_map/dot_general | solution.py:69
  165.9 0.0 all-reduce.4.cloned.1.call-update
  165.9 0.1 convert_reduce_fusion
  166.0 0.1 select_reduce_fusion
  166.1 37.3 %all-reduce.4.cloned.1.call-done = (f32[256,256]{1,0:T(8,128)}, f32[256,256]{1,0:T(8,128)}) async-done(((f32[256,256]{1,0:T(8,128)}, f32[256,256]{1,0:T(8,128)}), (f32[256,256]{1,0:T(8,128)}, f32[256,256]{1,0:T(8,128)})) %all-reduce.4.cloned.1.call-update) | async-done | bytes 524304 | tf_op jit(solution)/shard_map/psum | solution.py:70
  203.4 1.2 fusion.12
  204.7 2.0 fusion.15
  (11 shorter events, 0.1 us)
Async XLA Ops:
  6.5 12.0 %copy-start = (bf16[1,1024,256]{2,1,0:T(8,128)(2,1)S(1)}, bf16[1,1024,256]{2,1,0:T(8,128)(2,1)}, u32[]{:S(2)}) copy-start(bf16[1,1024,256]{2,1,0:T(8,128)(2,1)} %param.7) | copy-start | bytes 1572868
  6.5 13.1 %copy-start.1 = (bf16[1,1024,256]{2,1,0:T(8,128)(2,1)S(1)}, bf16[1,1024,256]{2,1,0:T(8,128)(2,1)}, u32[]{:S(2)}) copy-start(bf16[1,1024,256]{2,1,0:T(8,128)(2,1)} %param.8) | copy-start | bytes 1572868
  6.5 196.9 %all-reduce.4.cloned.1.call-start = ((), (), s32[]{:S(2)}) async-start(), calls=%async_computation | async-start | bytes 1048576 | tf_op jit(solution)/shard_map/psum | solution.py:70
Sparse Core Ops, SparseCore 0:
  166.0 37.3 all-reduce.3
